TPU v7x, 32 devices: a whole 2x2x4 slice. The times are simulated.
32 devices in a mesh: fsdp: 4 (over x, core), roll: 8 (over z, y).
Axes of the slice: x: 2, y: 2, z: 4, core: 2. Of those that a mesh axis runs over, the one named last changes fastest.
Arguments:
- trainer_weights: bfloat16 [8, 1024, 8192], P('roll', None, 'fsdp'), may hold values from -0.09375 to 0.09375
- power_table: int32 [8192, 512], P('fsdp'), may hold values from 1 to 250, as said below
- assign: int32 [2], replicated, may hold values from 0 to 7
Outputs:
- rollout_weights: bfloat16 [8, 2, 1024, 8192], P('roll', None, 'fsdp')
- fingerprint: bfloat16 [8, 2, 1024, 512], P('roll', None, 'fsdp')
Inputs may be any that keep to these rules, and one draw needn't show every extreme that they name: `power_table`: each entry is, modulo 251, a row factor times a column factor times the column's generator raised to the row index.
All inputs are finite; a program needn't handle non-finite values.
Results may differ from a plain program's by a relative error of at most 0.019.
Values may be sent and summed in bfloat16 or wider, within the bound.
A program may use at most 64 MiB of HBM per device.

v0:
```python
import jax
import jax.numpy as jnp
from jax import lax
from jax.sharding import PartitionSpec as P

spread_inverse = 1.0 / 72.0


def spread(block, axis, source):
    block = jnp.where(lax.axis_index(axis) == source, block, jnp.zeros_like(block))
    return lax.psum(block, axis)


def on_device(trainer_weights, power_table, assign):
    own_block = trainer_weights[0]
    centered = (power_table - 125).astype(jnp.bfloat16)
    layer_count = assign.shape[0]
    rollout_list = []
    printed_list = []
    regrouped = lax.all_to_all(own_block, "fsdp", split_axis=0, concat_axis=1, tiled=True)
    summed = lax.psum_scatter(
        jnp.dot(own_block, centered, preferred_element_type=jnp.float32).astype(jnp.bfloat16),
        "fsdp",
        scatter_dimension=0,
        tiled=True,
    ).astype(jnp.float32)
    printed = (summed * spread_inverse).astype(jnp.bfloat16)
    for number in range(layer_count):
        got_slice, got_print = (
            spread(regrouped, "roll", assign[number]),
            spread(printed, "roll", assign[number]),
        )
        rollout_list.append(got_slice)
        printed_list.append(got_print)
    return (jnp.stack(rollout_list)[None], jnp.stack(printed_list)[None])


def solution(mesh):
    in_specs = (P("roll", None, "fsdp"), P("fsdp", None), P())
    out_specs = (P("roll", None, "fsdp", None), P("roll", None, "fsdp", None))
    return jax.shard_map(
        on_device, mesh=mesh, in_specs=in_specs, out_specs=out_specs, check_vma=False
    )
```

profile of v0, /device:TPU:0, one launch (start us, length us, event | category | flops | bytes accessed | tf_op | source)
XLA Modules:
  0.0 391.7 jit_solution(1754313292101600169)
XLA Ops:
  7.2 4.9 %all-to-all-start = ((bf16[4,256,2048]{2,1,0:T(8,128)(2,1)}), bf16[4,256,2048]{2,1,0:T(8,128)(2,1)}, u32[]{:S(2)}, u32[]{:S(2)}) async-start(bf16[4,256,2048]{2,1,0:T(8,128)(2,1)} %bitcast.28), calls=%async_computation | async-start | bytes 8388608 | tf_op jit(solution)/shard_map/all_to_all | solution.py:20
  12.0 0.0 copy-start.2
  12.0 0.0 reduce-scatter.2.cloned.1.call-start
  12.1 6.8 %fusion.6 = bf16[1024,512]{0,1:T(8,128)(2,1)} fusion(bf16[1,1024,2048]{2,1,0:T(8,128)(2,1)} %param.3, s32[2048,512]{1,0:T(8,128)} %param.4), kind=kOutput, calls=%fused_computation.8 | convolution fusion | flops 2150105088 | bytes 9437184 | tf_op jit(solution)/shard_map/dot_general | solution.py:22
  18.9 0.0 reduce-scatter.2.cloned.1.call-update
  18.9 0.0 all-reduce.3.cloned.1.call-start
  19.0 0.0 copy-done.2
  19.0 0.6 fusion.10
  21.0 31.8 %reduce-scatter.2.cloned.1.call-done = bf16[256,512]{0,1:T(8,128)(2,1)} async-done(((bf16[1024,512]{0,1:T(8,128)(2,1)}), bf16[256,512]{0,1:T(8,128)(2,1)}) %reduce-scatter.2.cloned.1.call-update) | async-done | bytes 262160 | tf_op jit(solution)/shard_map/reduce_scatter | solution.py:21
  52.8 1.8 select_bitcast_fusion.1
  54.6 11.9 %all-to-all-done = bf16[4,256,2048]{2,1,0:T(8,128)(2,1)} async-done(((bf16[4,256,2048]{2,1,0:T(8,128)(2,1)}), bf16[4,256,2048]{2,1,0:T(8,128)(2,1)}, u32[]{:S(2)}, u32[]{:S(2)}) %all-to-all-start) | async-done | bytes 4194336 | tf_op jit(solution)/shard_map/all_to_all | solution.py:20
  66.5 6.2 %copy.8 = bf16[4,256,2048]{1,2,0:T(8,128)(2,1)} copy(bf16[4,256,2048]{2,1,0:T(8,128)(2,1)} %all-to-all-done) | data formatting | bytes 8388608 | tf_op jit(solution)/shard_map/all_to_all | solution.py:20
  72.7 6.1 %broadcast_select_fusion.1 = (bf16[4,256,2048]{1,2,0:T(8,128)(2,1)}, bf16[4,256,2048]{1,2,0:T(8,128)(2,1)}) fusion(bf16[4,256,2048]{1,2,0:T(8,128)(2,1)} %copy.8, pred[]{:T(512)S(6)} %eq.8, pred[]{:T(512)S(6)} %eq.9), kind=kLoop, calls=%fused_computation.5 | loop fusion | flops 4194304 | bytes 12582914 | tf_op jit(solution)/shard_map/jit(_where)/select_n | solution.py:10
  78.8 0.0 all-reduce.3.cloned.1.call-update
  78.8 285.5 %all-reduce.3.cloned.1.call-done = (bf16[1,256,8192]{1,2,0:T(8,128)(2,1)}, bf16[1,256,8192]{1,2,0:T(8,128)(2,1)}, bf16[1,256,512]{1,2,0:T(8,128)(2,1)}, bf16[1,256,512]{1,2,0:T(8,128)(2,1)}) async-done(((bf16[1,256,8192]{1,2,0:T(8,128)(2,1)}, bf16[1,256,8192]{1,2,0:T(8,128)(2,1)}, bf16[1,256,512]{1,2,0:T(8,128)(2,1)}, bf16[1,256,512]{1,2,0:T(8,128)(2,1)}), (bf16[1,256,8192]{1,2,0:T(8,128)(2,1)}, ...) | async-done | bytes 8912912 | tf_op jit(solution)/shard_map/psum | solution.py:11
  364.3 7.5 %maximum_bitcast_fusion = bf16[1,2,256,8192]{2,3,1,0:T(8,128)(2,1)} fusion(bf16[1,256,8192]{1,2,0:T(8,128)(2,1)} %get-tuple-element.8, bf16[1,256,8192]{1,2,0:T(8,128)(2,1)} %get-tuple-element.9), kind=kLoop, calls=%fused_computation | loop fusion | flops 4194304 | bytes 16777216 | tf_op jit(solution)/shard_map/broadcast_in_dim | solution.py:35
  371.8 0.0 copy-start
  371.8 0.0 copy-start.1
  371.8 12.0 %copy.10 = bf16[1,2,256,8192]{3,2,1,0:T(8,128)(2,1)} copy(bf16[1,2,256,8192]{2,3,1,0:T(8,128)(2,1)} %maximum_bitcast_fusion) | data formatting | bytes 16777216
  383.8 0.0 copy-done
  383.8 0.0 copy-done.1
  383.8 0.1 maximum_bitcast_fusion.1
  383.9 1.0 copy.11
Async XLA Ops:
  7.2 59.4 %all-to-all-start = ((bf16[4,256,2048]{2,1,0:T(8,128)(2,1)}), bf16[4,256,2048]{2,1,0:T(8,128)(2,1)}, u32[]{:S(2)}, u32[]{:S(2)}) async-start(bf16[4,256,2048]{2,1,0:T(8,128)(2,1)} %bitcast.28), calls=%async_computation | async-start | bytes 8388608 | tf_op jit(solution)/shard_map/all_to_all | solution.py:20
  12.0 7.0 %copy-start.2 = (s32[2]{0:T(128)S(1)}, s32[2]{0:T(128)}, u32[]{:S(2)}) copy-start(s32[2]{0:T(128)} %param.5) | copy-start | bytes 28
  12.0 40.7 %reduce-scatter.2.cloned.1.call-start = ((), (), s32[]{:S(2)}) async-start(), calls=%async_computation.2 | async-start | bytes 1310720 | tf_op jit(solution)/shard_map/reduce_scatter | solution.py:21
  18.9 345.4 %all-reduce.3.cloned.1.call-start = ((), (), s32[]{:S(2)}) async-start(), calls=%async_computation.3 | async-start | bytes 17825792 | tf_op jit(solution)/shard_map/psum | solution.py:11
  371.8 12.0 %copy-start = (bf16[1,256,512]{1,2,0:T(8,128)(2,1)S(1)}, bf16[1,256,512]{1,2,0:T(8,128)(2,1)}, u32[]{:S(2)}) copy-start(bf16[1,256,512]{1,2,0:T(8,128)(2,1)} %get-tuple-element.10) | copy-start | bytes 786436
  371.8 12.0 %copy-start.1 = (bf16[1,256,512]{1,2,0:T(8,128)(2,1)S(1)}, bf16[1,256,512]{1,2,0:T(8,128)(2,1)}, u32[]{:S(2)}) copy-start(bf16[1,256,512]{1,2,0:T(8,128)(2,1)} %get-tuple-element.11) | copy-start | bytes 786436
Sparse Core Ops, SparseCore 0:
  19.1 33.6 reduce-scatter.1
  78.9 285.3 all-reduce.2
where the time goes:
time: 392 us
  waiting for transfers between devices  329 us (84%)
  local copies, waits for them, and re-layouts  19.9 us (5%)
  other arithmetic  15.4 us (4%)
  between operations  15.4 us (4%)
  matrix products  6.83 us (2%)
  starting transfers between devices  4.94 us (1%)
    psum x1, waiting for transfers between devices, spread(): return lax.psum(block, axis)  286 us
    reduce_scatter x1, waiting for transfers between devices, on_device(): lax.psum_scatter(jnp.dot(own_block, centered, preferred_element_type=jnp....  31.8 us
    unnamed x8, local copies, waits for them, and re-layouts  13 us
    all_to_all x1, waiting for transfers between devices, on_device(): lax.all_to_all(own_block, 'fsdp', split_axis=0, concat_axis=1, tiled=True)  11.9 us
  transfers between devices with their start and end apart: 3, of which 3 were waited for; matrix products, arithmetic and copies ran while one was open for 2% of the time, Pallas kernels for 0%

commit v1 on v0

v1 whole, which is shorter than its diff:
```python
import functools

import jax
import jax.numpy as jnp
from jax import lax
from jax.experimental import pallas as pl
from jax.experimental.pallas import tpu as pltpu
from jax.sharding import PartitionSpec as P

spread_inverse = 1.0 / 72.0
CHUNKS = 8
MOST_SOURCES = 16
MESH = pl.DeviceIdType.MESH


def flip(index, mask):
    bit = 1
    while bit <= mask:
        if mask & bit:
            index = index + bit - 2 * bit * ((index // bit) % 2)
        bit *= 2
    return index


def powers_below(limit):
    bit, found = 1, []
    while bit < limit:
        found.append(bit)
        bit *= 2
    return found


def broadcast_kernel(n_roll, n_fsdp, source, chunks, with_table, *refs):
    if with_table:
        (w_ref, tab_ref, out_ref, all_ref, stage, local_sem, recv_sem, send_sem, swap_sem, t_local, t_recv, t_send) = refs
    else:
        w_ref, out_ref, stage, local_sem, recv_sem, send_sem, swap_sem = refs
    r, f = lax.axis_index("roll"), lax.axis_index("fsdp")
    half, rungs = n_fsdp // 2, n_roll // 2
    k, b = r // 2, r % 2
    ks, bs = source // 2, source % 2
    pivot = 2 * ks + 1 - bs
    inner = ks + 1 if ks + 1 < rungs else ks - 1
    relay = 2 * inner + 1 - bs
    rows, depth = out_ref.shape[0], w_ref.shape[1]
    height = rows // chunks
    is_source = r == source

    def piece(stream, c, i):
        owner = flip(f, stream * half + i)
        return out_ref.at[
            pl.ds(pl.multiple_of(c * height, height), height),
            pl.ds(pl.multiple_of(owner * depth, 128), depth),
        ]

    def mine(c, owner):
        return w_ref.at[pl.ds(pl.multiple_of(owner * rows + c * height, height), height), :]

    def move(stream, c, i, slot, to, own=False):
        q = c * half + i
        return pltpu.make_async_remote_copy(
            src_ref=mine(c, f) if own else piece(stream, c, i),
            dst_ref=piece(stream, c, i),
            send_sem=send_sem.at[stream, slot, q],
            recv_sem=recv_sem.at[stream, q],
            device_id={"roll": to, "fsdp": f},
            device_id_type=MESH,
        )

    def swap(c, m):
        peer = flip(f, m)
        dst = out_ref.at[
            pl.ds(pl.multiple_of(c * height, height), height),
            pl.ds(pl.multiple_of(f * depth, 128), depth),
        ]
        return pltpu.make_async_remote_copy(
            src_ref=mine(c, peer),
            dst_ref=dst,
            send_sem=swap_sem.at[m - 1, c],
            recv_sem=recv_sem.at[m // half, c * half + m % half],
            device_id={"roll": r, "fsdp": peer},
            device_id_type=MESH,
        )

    def arrived(stream, c, i):
        move(stream, c, i, 0, r).wait_recv()

    def each(body, count=chunks):
        def step(c, carry):
            body(c)
            return carry

        lax.fori_loop(0, count, step, 0)

    up = jnp.logical_and(k >= ks, k + 1 < rungs)
    down = jnp.logical_and(k <= ks, k >= 1)

    t_rows = depth // chunks

    def t_block(c, owner):
        return all_ref.at[pl.ds(pl.multiple_of(owner * depth + c * t_rows, t_rows), t_rows), :]

    def t_move(c, m, slot, to_roll, to_fsdp, m_there):
        owner = flip(f, m)
        src = tab_ref.at[pl.ds(pl.multiple_of(c * t_rows, t_rows), t_rows), :] if m == 0 else t_block(c, owner)
        return pltpu.make_async_remote_copy(
            src_ref=src,
            dst_ref=t_block(c, owner),
            send_sem=t_send.at[m, slot, c],
            recv_sem=t_recv.at[m_there, c],
            device_id={"roll": to_roll, "fsdp": to_fsdp},
            device_id_type=MESH,
        )

    bits = powers_below(n_fsdp)

    def t_own(c, finish):
        for slot, e in enumerate(bits):
            def go(e=e, slot=slot):
                copy = t_move(c, 0, slot, r, flip(f, e), e)
                copy.wait_send() if finish else copy.start()

            if e == half:
                pl.when(jnp.logical_not(is_source))(go)
            else:
                go()

    def t_pass(c, finish):
        for m in range(1, n_fsdp):
            if not finish:
                t_move(c, m, 0, r, f, m).wait_recv()
            for slot, e in enumerate(powers_below(m & -m)):
                copy = t_move(c, m, slot, r, flip(f, e), m + e)
                copy.wait_send() if finish else copy.start()
            if m == half:

                @pl.when(r == pivot)
                def _():
                    copy = t_move(c, m, len(bits), source, f, m)
                    copy.wait_send() if finish else copy.start()

    lag = 2

    def table_step(c):
        if with_table:

            @pl.when(c >= lag)
            def _():
                t_pass(c - lag, False)

    if with_table:
        keep = pltpu.make_async_copy(
            tab_ref, all_ref.at[pl.ds(pl.multiple_of(f * depth, depth), depth), :], t_local
        )
        keep.start()

    @pl.when(is_source)
    def _():
        load = pltpu.make_async_copy(w_ref.at[pl.ds(pl.multiple_of(f * rows, rows), rows), :], stage, local_sem.at[0])
        store = pltpu.make_async_copy(stage, out_ref.at[:, pl.ds(pl.multiple_of(f * depth, 128), depth)], local_sem.at[1])
        load.start()
        ways = ([(0, source + 2)] if ks + 1 < rungs else []) + ([(1, source - 2)] if ks >= 1 else [])

        def begin(c):
            for m in list(range(half, n_fsdp)) + list(range(1, half)):
                swap(c, m).start()
            for slot, to in ways:
                move(0, c, 0, slot, to, own=True).start()
            if with_table:
                t_own(c, False)

        each(begin)

        def step(c):
            for i in range(1, half):
                arrived(0, c, i)
                for slot, to in ways:
                    move(0, c, i, slot, to).start()
            for i in range(half):
                arrived(1, c, i)
                move(1, c, i, 2, pivot).start()
            table_step(c)

        each(step)
        load.wait()
        store.start()
        store.wait()

        def finish(c):
            for m in range(1, n_fsdp):
                swap(c, m).wait_send()
            for slot, to in ways:
                for i in range(half):
                    move(0, c, i, slot, to, own=i == 0).wait_send()
            for i in range(half):
                move(1, c, i, 2, pivot).wait_send()

        each(finish)

    def carry_on(stream, c, i, finish):
        def do(slot, to):
            copy = move(stream, c, i, slot, to)
            copy.wait_send() if finish else copy.start()

        pl.when(up)(lambda: do(0, r + 2))
        pl.when(down)(lambda: do(1, r - 2))
        pl.when(k != ks)(lambda: do(2, r + 1 - 2 * b))

    @pl.when(jnp.logical_not(is_source))
    def _():
        if with_table:
            each(lambda c: t_own(c, False))

    @pl.when(jnp.logical_and(b == bs, k != ks))
    def _():
        def step(c):
            for i in range(half):
                arrived(0, c, i)
                carry_on(0, c, i, False)
            table_step(c)

        each(step)

        def finish(c):
            for i in range(half):
                arrived(1, c, i)
                carry_on(0, c, i, True)

        each(finish)

    @pl.when(b != bs)
    def _():
        def step(c):
            for i in range(half):

                @pl.when(r == relay)
                def _():
                    arrived(0, c, i)
                    move(0, c, i, 0, pivot).start()

                arrived(1, c, i)
                carry_on(1, c, i, False)
            table_step(c)

        each(step)

        def finish(c):
            for i in range(half):

                @pl.when(r == relay)
                def _():
                    move(0, c, i, 0, pivot).wait_send()

                @pl.when(r != relay)
                def _():
                    arrived(0, c, i)

                carry_on(1, c, i, True)

        each(finish)

    if with_table:
        each(lambda c: t_pass(c + chunks - lag, False), lag)

        def finish(c):
            t_own(c, True)
            t_pass(c, True)

        each(finish)
        keep.wait()


def broadcast(n_roll, n_fsdp, source, layer, own_block, table):
    rows, depth = own_block.shape[0] // n_fsdp, own_block.shape[1]
    half = n_fsdp // 2
    chunks = min(CHUNKS, rows // 16)
    with_table = table is not None
    anywhere = pl.BlockSpec(memory_space=pl.ANY)
    out_shape = [jax.ShapeDtypeStruct((rows, depth * n_fsdp), own_block.dtype)]
    in_specs = [anywhere]
    scratch = [
        pltpu.VMEM((rows, depth), own_block.dtype),
        pltpu.SemaphoreType.DMA((2,)),
        pltpu.SemaphoreType.DMA((2, chunks * half)),
        pltpu.SemaphoreType.DMA((2, 3, chunks * half)),
        pltpu.SemaphoreType.DMA((n_fsdp - 1, chunks)),
    ]
    operands = [own_block]
    if with_table:
        out_shape.append(jax.ShapeDtypeStruct((depth * n_fsdp, table.shape[1]), table.dtype))
        in_specs.append(pl.BlockSpec(memory_space=pltpu.VMEM))
        scratch += [
            pltpu.SemaphoreType.DMA,
            pltpu.SemaphoreType.DMA((n_fsdp, chunks)),
            pltpu.SemaphoreType.DMA((n_fsdp, len(powers_below(n_fsdp)) + 1, chunks)),
        ]
        operands.append(table)
    return pl.pallas_call(
        functools.partial(broadcast_kernel, n_roll, n_fsdp, source, chunks, with_table),
        out_shape=out_shape,
        in_specs=in_specs,
        out_specs=[anywhere] * len(out_shape),
        scratch_shapes=scratch,
        name=f"broadcast_{layer}_{source}",
        compiler_params=pltpu.CompilerParams(has_side_effects=True),
    )(*operands)


def spread(block, axis, source):
    block = jnp.where(lax.axis_index(axis) == source, block, jnp.zeros_like(block))
    return lax.psum(block, axis)


def by_sums(own_block, centered, assign):
    regrouped = lax.all_to_all(own_block, "fsdp", split_axis=0, concat_axis=1, tiled=True)
    summed = lax.psum_scatter(
        jnp.dot(own_block, centered, preferred_element_type=jnp.float32).astype(jnp.bfloat16),
        "fsdp",
        scatter_dimension=0,
        tiled=True,
    ).astype(jnp.float32)
    printed = (summed * spread_inverse).astype(jnp.bfloat16)
    layers = range(assign.shape[0])
    return (
        jnp.stack([spread(regrouped, "roll", assign[number]) for number in layers])[None],
        jnp.stack([spread(printed, "roll", assign[number]) for number in layers])[None],
    )


def on_device(n_roll, n_fsdp, trainer_weights, power_table, assign):
    own_block = trainer_weights[0]
    centered = (power_table - 125).astype(jnp.bfloat16)
    if n_roll > MOST_SOURCES or n_roll < 4 or n_roll % 2 or n_fsdp & (n_fsdp - 1) or n_fsdp < 2:
        return by_sums(own_block, centered, assign)
    got, table = [], None
    for number in range(assign.shape[0]):
        branches = [
            functools.partial(broadcast, n_roll, n_fsdp, source, number) for source in range(n_roll)
        ]
        if number == 0:
            piece, table = lax.switch(assign[number], branches, own_block, centered)
        else:
            (piece,) = lax.switch(
                assign[number], [functools.partial(lambda g, w: g(w, None), g) for g in branches], own_block
            )
        got.append(piece)
    rollout = jnp.stack(got)
    printed = jnp.einsum("lcd,df->lcf", rollout, table, preferred_element_type=jnp.float32)
    return rollout[None], (printed * spread_inverse).astype(jnp.bfloat16)[None]


def solution(mesh):
    in_specs = (P("roll", None, "fsdp"), P("fsdp", None), P())
    out_specs = (P("roll", None, "fsdp", None), P("roll", None, "fsdp", None))
    return jax.shard_map(
        functools.partial(on_device, mesh.shape["roll"], mesh.shape["fsdp"]),
        mesh=mesh, in_specs=in_specs, out_specs=out_specs, check_vma=False,
    )
```

time: 392 us -> 248 us (0.63)
  waiting for transfers between devices: 329 us -> 0 us
  Pallas kernels: 0 us -> 225 us
  local copies, waits for them, and re-layouts: 19.9 us -> 0.59 us
  between operations: 15.4 us -> 1.98 us
  other arithmetic: 15.4 us -> 9.12 us
  starting transfers between devices: 4.94 us -> 0 us
  matrix products: 6.83 us -> 11.3 us
    psum x1 -> x0, waiting for transfers between devices: 286 us -> none  [spread(): return lax.psum(block, axis)]
    pallas_call x0 -> x2, Pallas kernels: none -> 225 us  [broadcast(): pl.pallas_call(functools.partial(broadcast_kernel, n_roll, n_fsdp, source...]
    reduce_scatter x1 -> x0, waiting for transfers between devices: 31.8 us -> none  [on_device(): lax.psum_scatter(jnp.dot(own_block, centered, preferred_element_type=jnp....]
    unnamed x8 -> x4, local copies, waits for them, and re-layouts: 13 us -> 0.01 us
    all_to_all x1 -> x0, waiting for transfers between devices: 11.9 us -> none  [on_device(): lax.all_to_all(own_block, 'fsdp', split_axis=0, concat_axis=1, tiled=True)]
    all_to_all x1 -> x0, local copies, waits for them, and re-layouts: 6.18 us -> none  [on_device(): lax.all_to_all(own_block, 'fsdp', split_axis=0, concat_axis=1, tiled=True)]
    select_n x1 -> x0, other arithmetic: 6.06 us -> none  [spread(): jnp.where(lax.axis_index(axis) == source, block, jnp.zeros_like(block))]
    all_to_all x1 -> x0, starting transfers between devices: 4.85 us -> none  [on_device(): lax.all_to_all(own_block, 'fsdp', split_axis=0, concat_axis=1, tiled=True)]
  transfers between devices with their start and end apart: 3 -> 0, of which waited for: 3 -> 0; matrix products, arithmetic and copies ran while one was open for 2% -> 0% of each run, Pallas kernels for 0% -> 0%
where the time goes in v1:
time: 248 us
  Pallas kernels  225 us (91%)
  matrix products  11.3 us (5%)
  other arithmetic  9.12 us (4%)
    pallas_call x2, Pallas kernels, broadcast(): pl.pallas_call(functools.partial(broadcast_kernel, n_roll, n_fsdp, source...  225 us
    dot_general x1, matrix products, on_device(): jnp.einsum('lcd,df->lcf', rollout, table, preferred_element_type=jnp.floa...  11.3 us
    broadcast_in_dim x1, other arithmetic, on_device(): rollout[None]  6.35 us

profile of v1, /device:TPU:0, one launch (start us, length us, event | category | flops | bytes accessed | tf_op | source)
XLA Modules:
  0.0 248.1 jit_solution(6682166165393559028)
XLA Ops:
  0.6 0.0 copy-start.1
  0.6 2.8 %add_convert_fusion = bf16[2048,512]{1,0:T(8,128)(2,1)S(1)} fusion(s32[2048,512]{1,0:T(8,128)} %param.20), kind=kLoop, calls=%fused_computation.4 | loop fusion | flops 2097152 | bytes 6291456 | tf_op jit(solution)/shard_map/convert_element_type | solution.py:332
  3.4 0.0 copy-done.1
  3.4 0.6 fusion.13
  4.7 142.9 %conditional.2 = (bf16[8192,512]{1,0:T(8,128)(2,1)}, bf16[1,256,8192]{2,1,0:T(8,128)(2,1)}) conditional(s32[]{:T(128)} %bitcast.16, (bf16[1024,2048]{1,0:T(8,128)(2,1)}, bf16[2048,512]{1,0:T(8,128)(2,1)S(1)}) %tuple.99, (bf16[1024,2048]{1,0:T(8,128)(2,1)}, bf16[2048,512]{1,0:T(8,128)(2,1)S(1)}) %tuple.100, ...), branch_computations={%region_0.0_spmd, %region_1.0_spmd, %region_2.0_spmd, %region_3.0_... | conditional | bytes 16 | solution.py:341
  4.7 142.8 %broadcast_0_0.1 = (bf16[256,8192]{1,0:T(8,128)(2,1)}, bf16[8192,512]{1,0:T(8,128)(2,1)}) custom-call(bf16[1024,2048]{1,0:T(8,128)(2,1)} %get-tuple-element.67.refs_0_, bf16[2048,512]{1,0:T(8,128)(2,1)S(1)} %get-tuple-element.68.refs_1_), custom_call_target="tpu_custom_call" | custom-call | tf_op jit(solution)/shard_map/cond/branch_0_fun/broadcast_0_0/pallas_call | solution.py:298
  148.2 82.2 %conditional.3 = (bf16[1,256,8192]{2,1,0:T(8,128)(2,1)}) conditional(s32[]{:T(128)} %bitcast.18, bf16[1024,2048]{1,0:T(8,128)(2,1)} %bitcast.40, bf16[1024,2048]{1,0:T(8,128)(2,1)} %bitcast.41, bf16[1024,2048]{1,0:T(8,128)(2,1)} %bitcast.42, bf16[1024,2048]{1,0:T(8,128)(2,1)} %bitcast.43, ...), branch_computations={%region_8.0_spmd, %region_9.0_spmd, %region_10.0_spmd, %region_11.... | conditional | bytes 8 | solution.py:343
  148.4 82.0 %broadcast_1_5.1 = bf16[256,8192]{1,0:T(8,128)(2,1)} custom-call(bf16[1024,2048]{1,0:T(8,128)(2,1)} %refs_0_.5), custom_call_target="tpu_custom_call" | custom-call | tf_op jit(solution)/shard_map/cond/branch_5_fun/broadcast_1_5/pallas_call | solution.py:298
  230.4 0.0 copy-start
  230.5 11.3 %fusion.9 = bf16[1,2,256,512]{3,2,1,0:T(8,128)(2,1)} fusion(bf16[8192,512]{1,0:T(8,128)(2,1)} %get-tuple-element.104, bf16[1,256,8192]{2,1,0:T(8,128)(2,1)} %get-tuple-element.123, bf16[1,256,8192]{2,1,0:T(8,128)(2,1)} %get-tuple-element.103), kind=kOutput, calls=%fused_computation.7 | convolution fusion | flops 4299685888 | bytes 17301504 | tf_op jit(solution)/shard_map/lcd,df->lcf/dot_general | solution.py:348
  241.7 0.0 copy-done
  241.7 6.3 %fusion.2 = bf16[1,2,256,8192]{3,2,1,0:T(8,128)(2,1)} fusion(bf16[1,256,8192]{2,1,0:T(8,128)(2,1)S(1)} %copy-done, bf16[1,256,8192]{2,1,0:T(8,128)(2,1)} %get-tuple-element.103), kind=kLoop, calls=%fused_computation.3 | loop fusion | flops 4194304 | bytes 16777216 | tf_op jit(solution)/shard_map/broadcast_in_dim | solution.py:349
Async XLA Ops:
  0.6 2.8 %copy-start.1 = (s32[2]{0:T(128)S(1)}, s32[2]{0:T(128)}, u32[]{:S(2)}) copy-start(s32[2]{0:T(128)} %param.21) | copy-start | bytes 28
  230.4 11.3 %copy-start = (bf16[1,256,8192]{2,1,0:T(8,128)(2,1)S(1)}, bf16[1,256,8192]{2,1,0:T(8,128)(2,1)}, u32[]{:S(2)}) copy-start(bf16[1,256,8192]{2,1,0:T(8,128)(2,1)} %get-tuple-element.123) | copy-start | bytes 12582916

commit v2 on v1

--- a/solution.py
+++ b/solution.py
@@ -8,7 +8,7 @@
 from jax.sharding import PartitionSpec as P
 
 spread_inverse = 1.0 / 72.0
-CHUNKS = 8
+CHUNKS = 16
 MOST_SOURCES = 16
 MESH = pl.DeviceIdType.MESH
 
@@ -270,7 +270,7 @@
         keep.wait()
 
 
-def broadcast(n_roll, n_fsdp, source, layer, own_block, table):
+def broadcast(n_roll, n_fsdp, source, layer, own_block, table=None):
     rows, depth = own_block.shape[0] // n_fsdp, own_block.shape[1]
     half = n_fsdp // 2
     chunks = min(CHUNKS, rows // 16)
@@ -327,26 +327,62 @@
     )
 
 
+def assemble_kernel(n_fsdp, depth, *refs):
+    *got_refs, rollout_ref, printed_ref, total = refs
+    step = pl.program_id(1)
+    for layer, got_ref in enumerate(got_refs):
+        rollout_ref[layer] = got_ref[:, :depth]
+        term = got_ref[:, depth:].astype(jnp.float32)
+
+        @pl.when(step == 0)
+        def _():
+            total[layer] = term
+
+        @pl.when(step > 0)
+        def _():
+            total[layer] += term
+
+        @pl.when(step == n_fsdp - 1)
+        def _():
+            printed_ref[layer] = (total[layer] * spread_inverse).astype(jnp.bfloat16)
+
+
+def assemble(got, n_fsdp, depth, width):
+    layers, rows = len(got), got[0].shape[0]
+    tile = rows // 2
+    return pl.pallas_call(
+        functools.partial(assemble_kernel, n_fsdp, depth),
+        grid=(rows // tile, n_fsdp),
+        in_specs=[pl.BlockSpec((tile, depth + width), lambda i, j: (i, j))] * layers,
+        out_specs=[
+            pl.BlockSpec((layers, tile, depth), lambda i, j: (0, i, j)),
+            pl.BlockSpec((layers, tile, width), lambda i, j: (0, i, 0)),
+        ],
+        out_shape=[
+            jax.ShapeDtypeStruct((layers, rows, depth * n_fsdp), jnp.bfloat16),
+            jax.ShapeDtypeStruct((layers, rows, width), jnp.bfloat16),
+        ],
+        scratch_shapes=[pltpu.VMEM((layers, tile, width), jnp.float32)],
+        name="assemble",
+    )(*got)
+
+
 def on_device(n_roll, n_fsdp, trainer_weights, power_table, assign):
     own_block = trainer_weights[0]
     centered = (power_table - 125).astype(jnp.bfloat16)
     if n_roll > MOST_SOURCES or n_roll < 4 or n_roll % 2 or n_fsdp & (n_fsdp - 1) or n_fsdp < 2:
         return by_sums(own_block, centered, assign)
-    got, table = [], None
+    depth, width = own_block.shape[1], centered.shape[1]
+    partial = jnp.dot(own_block, centered, preferred_element_type=jnp.float32).astype(jnp.bfloat16)
+    joined = jnp.concatenate([own_block, partial], axis=1)
+    got = []
     for number in range(assign.shape[0]):
         branches = [
             functools.partial(broadcast, n_roll, n_fsdp, source, number) for source in range(n_roll)
         ]
-        if number == 0:
-            piece, table = lax.switch(assign[number], branches, own_block, centered)
-        else:
-            (piece,) = lax.switch(
-                assign[number], [functools.partial(lambda g, w: g(w, None), g) for g in branches], own_block
-            )
-        got.append(piece)
-    rollout = jnp.stack(got)
-    printed = jnp.einsum("lcd,df->lcf", rollout, table, preferred_element_type=jnp.float32)
-    return rollout[None], (printed * spread_inverse).astype(jnp.bfloat16)[None]
+        got.append(lax.switch(assign[number], branches, joined)[0])
+    rollout, printed = assemble(got, n_fsdp, depth, width)
+    return rollout[None], printed[None]
 
 
 def solution(mesh):

time: 248 us -> 237 us (0.956); the launches traced: 248 us -> 234 us
  Pallas kernels: 225 us -> 219 us
  matrix products: 11.3 us -> 5.85 us
  other arithmetic: 9.12 us -> 4.97 us
    pallas_call x2, Pallas kernels: 225 us -> 209 us  [broadcast(): pl.pallas_call(functools.partial(broadcast_kernel, n_roll, n_fsdp, source...]
    pallas_call x0 -> x1, Pallas kernels: none -> 9.73 us  [assemble(): pl.pallas_call(functools.partial(assemble_kernel, n_fsdp, depth), grid=(r...]
    broadcast_in_dim x1 -> x0, other arithmetic: 6.35 us -> none  [on_device(): rollout[None]]
    dot_general x1, matrix products: 11.3 us -> 5.85 us  [on_device(): jnp.dot(own_block, centered, preferred_element_type=jnp.float32)]
    concatenate x0 -> x1, other arithmetic: none -> 4.97 us  [on_device(): joined = jnp.concatenate([own_block, partial], axis=1)]
    convert_element_type x1 -> x0, other arithmetic: 2.77 us -> none  [on_device(): centered = (power_table - 125).astype(jnp.bfloat16)]
where the time goes in v2:
time: 237 us; the launch traced here: 234 us
  Pallas kernels  219 us (92%)
  matrix products  5.85 us (2%)
  other arithmetic  4.97 us (2%)
    pallas_call x2, Pallas kernels, broadcast(): pl.pallas_call(functools.partial(broadcast_kernel, n_roll, n_fsdp, source...  209 us
    pallas_call x1, Pallas kernels, assemble(): pl.pallas_call(functools.partial(assemble_kernel, n_fsdp, depth), grid=(r...  9.73 us
    dot_general x1, matrix products, on_device(): jnp.dot(own_block, centered, preferred_element_type=jnp.float32)  5.85 us
    concatenate x1, other arithmetic, on_device(): joined = jnp.concatenate([own_block, partial], axis=1)  4.97 us

profile of v2, /device:TPU:0, one launch (start us, length us, event | category | flops | bytes accessed | tf_op | source)
XLA Modules:
  0.0 234.0 jit_solution(8692944204844260978)
XLA Ops:
  0.6 1.3 fusion.6
  3.2 5.9 %fusion.3 = bf16[1024,512]{0,1:T(8,128)(2,1)S(1)} fusion(s32[2048,512]{1,0:T(8,128)} %param.20, bf16[1,1024,2048]{2,1,0:T(8,128)(2,1)} %param.19), kind=kOutput, calls=%fused_computation.5 | convolution fusion | flops 2150105088 | bytes 9437184 | tf_op jit(solution)/shard_map/dot_general | solution.py:376
  9.1 0.5 copy.5
  9.7 5.0 %pad_maximum_fusion = bf16[1024,2560]{1,0:T(8,128)(2,1)} fusion(bf16[1024,512]{1,0:T(8,128)(2,1)S(1)} %copy.5, bf16[1024,2048]{1,0:T(8,128)(2,1)} %bitcast.9), kind=kLoop, calls=%fused_computation | loop fusion | flops 10485760 | bytes 10485760 | tf_op jit(solution)/shard_map/concatenate | solution.py:377
  14.6 72.2 %conditional.3 = (bf16[256,10240]{1,0:T(8,128)(2,1)}) conditional(s32[]{:T(128)} %bitcast.3, bf16[1024,2560]{1,0:T(8,128)(2,1)} %pad_maximum_fusion, bf16[1024,2560]{1,0:T(8,128)(2,1)} %pad_maximum_fusion, bf16[1024,2560]{1,0:T(8,128)(2,1)} %pad_maximum_fusion, bf16[1024,2560]{1,0:T(8,128)(2,1)} %pad_maximum_fusion, ...), branch_computations={%region_8.0_spmd, %region_9.0_spmd, %region_10.0_spmd, %region_11.... | conditional | bytes 8 | solution.py:383
  14.6 72.0 %broadcast_1_0.1 = bf16[256,10240]{1,0:T(8,128)(2,1)} custom-call(bf16[1024,2560]{1,0:T(8,128)(2,1)} %refs_0_.8), custom_call_target="tpu_custom_call" | custom-call | tf_op jit(solution)/shard_map/cond/branch_0_fun/broadcast_1_0/pallas_call | solution.py:298
  86.9 137.4 %conditional.2 = (bf16[256,10240]{1,0:T(8,128)(2,1)}) conditional(s32[]{:T(128)} %bitcast, bf16[1024,2560]{1,0:T(8,128)(2,1)} %pad_maximum_fusion, bf16[1024,2560]{1,0:T(8,128)(2,1)} %pad_maximum_fusion, bf16[1024,2560]{1,0:T(8,128)(2,1)} %pad_maximum_fusion, bf16[1024,2560]{1,0:T(8,128)(2,1)} %pad_maximum_fusion, ...), branch_computations={%region_0.0_spmd, %region_1.0_spmd, %region_2.0_spmd, %region_3.0_... | conditional | bytes 8 | solution.py:383
  86.9 137.4 %broadcast_0_1.1 = bf16[256,10240]{1,0:T(8,128)(2,1)} custom-call(bf16[1024,2560]{1,0:T(8,128)(2,1)} %refs_0_.1), custom_call_target="tpu_custom_call" | custom-call | tf_op jit(solution)/shard_map/cond/branch_1_fun/broadcast_0_1/pallas_call | solution.py:298
  224.3 9.7 %assemble.1 = (bf16[2,256,8192]{2,1,0:T(8,128)(2,1)}, bf16[2,256,512]{2,1,0:T(8,128)(2,1)}) custom-call(bf16[256,10240]{1,0:T(8,128)(2,1)} %get-tuple-element.42.refs_0_, bf16[256,10240]{1,0:T(8,128)(2,1)} %get-tuple-element.43.refs_1_), custom_call_target="tpu_custom_call" | custom-call | tf_op jit(solution)/shard_map/assemble/pallas_call | solution.py:353

commit v3 on v2

--- a/solution.py
+++ b/solution.py
@@ -169,9 +169,11 @@
             if with_table:
                 t_own(c, False)
 
-        each(begin)
+        lead = min(3, chunks)
+        each(begin, lead)
 
         def step(c):
+            pl.when(c + lead < chunks)(lambda: begin(c + lead))
             for i in range(1, half):
                 arrived(0, c, i)
                 for slot, to in ways:

time: 237 us -> 199 us (0.84); the launches traced: 234 us -> 203 us
  Pallas kernels: 219 us -> 188 us
    pallas_call x2, Pallas kernels: 209 us -> 178 us  [broadcast(): pl.pallas_call(functools.partial(broadcast_kernel, n_roll, n_fsdp, source...]
where the time goes in v3:
time: 199 us; the launch traced here: 203 us
  Pallas kernels  188 us (94%)
  matrix products  5.85 us (3%)
  other arithmetic  4.97 us (2%)
    pallas_call x2, Pallas kernels, broadcast(): pl.pallas_call(functools.partial(broadcast_kernel, n_roll, n_fsdp, source...  178 us
    pallas_call x1, Pallas kernels, assemble(): pl.pallas_call(functools.partial(assemble_kernel, n_fsdp, depth), grid=(r...  9.73 us
    dot_general x1, matrix products, on_device(): jnp.dot(own_block, centered, preferred_element_type=jnp.float32)  5.85 us
    concatenate x1, other arithmetic, on_device(): joined = jnp.concatenate([own_block, partial], axis=1)  4.97 us

profile of v3, /device:TPU:0, one launch (start us, length us, event | category | flops | bytes accessed | tf_op | source)
XLA Modules:
  0.0 202.6 jit_solution(2128600309922952366)
XLA Ops:
  0.6 1.3 fusion.6
  3.2 5.9 %fusion.3 = bf16[1024,512]{0,1:T(8,128)(2,1)S(1)} fusion(s32[2048,512]{1,0:T(8,128)} %param.20, bf16[1,1024,2048]{2,1,0:T(8,128)(2,1)} %param.19), kind=kOutput, calls=%fused_computation.5 | convolution fusion | flops 2150105088 | bytes 9437184 | tf_op jit(solution)/shard_map/dot_general | solution.py:378
  9.1 0.5 copy.5
  9.7 5.0 %pad_maximum_fusion = bf16[1024,2560]{1,0:T(8,128)(2,1)} fusion(bf16[1024,512]{1,0:T(8,128)(2,1)S(1)} %copy.5, bf16[1024,2048]{1,0:T(8,128)(2,1)} %bitcast.9), kind=kLoop, calls=%fused_computation | loop fusion | flops 10485760 | bytes 10485760 | tf_op jit(solution)/shard_map/concatenate | solution.py:379
  14.6 90.8 %conditional.3 = (bf16[256,10240]{1,0:T(8,128)(2,1)}) conditional(s32[]{:T(128)} %bitcast.3, bf16[1024,2560]{1,0:T(8,128)(2,1)} %pad_maximum_fusion, bf16[1024,2560]{1,0:T(8,128)(2,1)} %pad_maximum_fusion, bf16[1024,2560]{1,0:T(8,128)(2,1)} %pad_maximum_fusion, bf16[1024,2560]{1,0:T(8,128)(2,1)} %pad_maximum_fusion, ...), branch_computations={%region_8.0_spmd, %region_9.0_spmd, %region_10.0_spmd, %region_11.... | conditional | bytes 8 | solution.py:385
  14.6 90.6 %broadcast_1_7.1 = bf16[256,10240]{1,0:T(8,128)(2,1)} custom-call(bf16[1024,2560]{1,0:T(8,128)(2,1)} %refs_0_.15), custom_call_target="tpu_custom_call" | custom-call | tf_op jit(solution)/shard_map/cond/branch_7_fun/broadcast_1_7/pallas_call | solution.py:300
  105.4 87.4 %conditional.2 = (bf16[256,10240]{1,0:T(8,128)(2,1)}) conditional(s32[]{:T(128)} %bitcast, bf16[1024,2560]{1,0:T(8,128)(2,1)} %pad_maximum_fusion, bf16[1024,2560]{1,0:T(8,128)(2,1)} %pad_maximum_fusion, bf16[1024,2560]{1,0:T(8,128)(2,1)} %pad_maximum_fusion, bf16[1024,2560]{1,0:T(8,128)(2,1)} %pad_maximum_fusion, ...), branch_computations={%region_0.0_spmd, %region_1.0_spmd, %region_2.0_spmd, %region_3.0_... | conditional | bytes 8 | solution.py:385
  105.4 87.4 %broadcast_0_6.1 = bf16[256,10240]{1,0:T(8,128)(2,1)} custom-call(bf16[1024,2560]{1,0:T(8,128)(2,1)} %refs_0_.6), custom_call_target="tpu_custom_call" | custom-call | tf_op jit(solution)/shard_map/cond/branch_6_fun/broadcast_0_6/pallas_call | solution.py:300
  192.8 9.7 %assemble.1 = (bf16[2,256,8192]{2,1,0:T(8,128)(2,1)}, bf16[2,256,512]{2,1,0:T(8,128)(2,1)}) custom-call(bf16[256,10240]{1,0:T(8,128)(2,1)} %get-tuple-element.42.refs_0_, bf16[256,10240]{1,0:T(8,128)(2,1)} %get-tuple-element.43.refs_1_), custom_call_target="tpu_custom_call" | custom-call | tf_op jit(solution)/shard_map/assemble/pallas_call | solution.py:355
